TPU v7x, 256 devices: a whole 4x4x8 slice. The times are simulated.
256 devices in a mesh: seq: 16 (over z_hi, x), dp: 8 (over y, core), head: 2 (over z_lo).
Axes of the slice: x: 4, y: 4, z: 8 (z_hi: 4, z_lo: 2; z = z_hi * 2 + z_lo), core: 2. Of those that a mesh axis runs over, the one named last changes fastest.
Arguments:
- queries: bfloat16 [8, 2048, 2048], P('dp', 'seq', 'head'), may hold values from -5 to 5
- keys: bfloat16 [8, 2048, 512], P('dp', 'seq', 'head'), may hold values from -5 to 5
- values: bfloat16 [8, 2048, 512], P('dp', 'seq', 'head'), may hold values from -4 to 4
- query_tangent: bfloat16 [8, 2048, 2048], P('dp', 'seq', 'head'), may hold values from -4 to 4
- key_tangent: bfloat16 [8, 2048, 512], P('dp', 'seq', 'head'), may hold values from -4 to 4
- value_tangent: bfloat16 [8, 2048, 512], P('dp', 'seq', 'head'), may hold values from -4 to 4
- lengths: int32 [8, 17], P('dp'), may hold values from 0 to 256, as said below
- out_weight: bfloat16 [2048, 4096], P('head'), may hold values from -0.125 to 0.125
- cotangent: bfloat16 [8, 2048, 4096], P('dp', 'seq'), may hold values from -0.0625 to 0.0625
Outputs:
- layer_tangent: bfloat16 [8, 2048, 4096], P('dp', 'seq', 'head')
- weight_hvp: float32 [4096, 2048], P(('seq', 'dp'), 'head')
Inputs may be any that keep to these rules, and one draw needn't show every extreme that they name: `lengths`: each row sums to 2048; a length may be 0; in every row some document has exactly 256 tokens.
All inputs are finite; a program needn't handle non-finite values.
Results may differ from a plain program's by a relative error of at most 0.014.
Values may be sent and summed in bfloat16 or wider, within the bound.
A program may use at most 128 MiB of HBM per device.

v0:
```python
import jax
import jax.numpy as jnp
from jax import lax
from jax.sharding import PartitionSpec as P

HEADS = 16
KV_HEADS = 4
HEAD_DIM = 128
DOC_SHARDS = 2


def from_behind(block, axis, distance):
    devices = range(lax.axis_size(axis))
    route = [(i - distance, i) for i in devices if i - distance in devices]
    return lax.ppermute(block, axis, route)


def in_blocks(array, dim, length):
    dims = array.shape
    pieces = array.reshape(*dims[:dim], length, dims[dim] // length, *dims[dim + 1 :])
    return jnp.moveaxis(pieces, dim, 0)


def sent_and_summed(array, axis, dim):
    length = lax.axis_size(axis)
    pieces = lax.all_to_all(in_blocks(array, dim, length), axis, 0, 0, tiled=True)
    return jnp.sum(pieces.astype(jnp.float32), axis=0)


def doc_numbers(lengths_row, count):
    ends = jnp.cumsum(lengths_row)
    positions = jnp.arange(count, dtype=jnp.int32)
    return jnp.sum((ends[None, :] <= positions[:, None]).astype(jnp.int32), axis=1)


def on_device(
    queries, keys, values, query_tangent, key_tangent, value_tangent, lengths, out_weight, cotangent
):
    tok_count = queries.shape[1]
    seq_count = lax.axis_size("seq")
    shard_index = lax.axis_index("seq")
    whole_len = tok_count * seq_count
    group_ratio = HEADS // KV_HEADS
    groups = keys.shape[2] // HEAD_DIM
    score_scale = HEAD_DIM ** (-0.5)
    doc_ids = doc_numbers(lengths[0], whole_len)
    query_first = shard_index * tok_count
    query_rows = queries[0].reshape(tok_count, groups, group_ratio, HEAD_DIM)
    dquery_rows = query_tangent[0].reshape(tok_count, groups, group_ratio, HEAD_DIM)
    packed = jnp.stack([keys[0], values[0], key_tangent[0], value_tangent[0]])

    def update(totals, query_block_rows, query_rows_gradient, qpos, qdocs, block_data, first_row):
        highest, total, cross, running_total, accum_tangent = totals
        block_len = block_data.shape[1]
        key_pos = first_row + jnp.arange(block_len, dtype=jnp.int32)
        key_docs = doc_ids[jnp.clip(key_pos, 0, whole_len - 1)]
        allowed = (
            (key_docs[None, :] == qdocs[:, None])
            & (key_pos[None, :] <= qpos[:, None])
            & (key_pos >= 0)[None, :]
        )
        key_slice = block_data[0].reshape(block_len, groups, HEAD_DIM)
        value_slice = block_data[1].reshape(block_len, groups, HEAD_DIM)
        key_slice_gradient = block_data[2].reshape(block_len, groups, HEAD_DIM)
        value_slice_gradient = block_data[3].reshape(block_len, groups, HEAD_DIM)
        both_queries = jnp.concatenate([query_block_rows, query_rows_gradient], axis=2)
        both_scores = jnp.einsum(
            "fmhc,omc->mhfo", both_queries, key_slice, preferred_element_type=jnp.float32
        )
        scores = both_scores[:, :group_ratio] * score_scale
        tangent = (
            both_scores[:, group_ratio:]
            + jnp.einsum(
                "fmhc,omc->mhfo",
                query_block_rows,
                key_slice_gradient,
                preferred_element_type=jnp.float32,
            )
        ) * score_scale
        scores = jnp.where(allowed, scores, -1e30)
        new_high = jnp.maximum(highest, jnp.max(scores, axis=-1))
        weight = jnp.where(allowed, jnp.exp(scores - new_high[..., None]), 0.0)
        weighted_tangent = weight * tangent
        fade = jnp.exp(highest - new_high)
        total = total * fade + jnp.sum(weight, axis=-1)
        cross = cross * fade + jnp.sum(weighted_tangent, axis=-1)
        lower_bound = weight.astype(jnp.bfloat16)
        lower_bound_tangent = weighted_tangent.astype(jnp.bfloat16)
        both_weights = jnp.concatenate([lower_bound, lower_bound_tangent], axis=1)
        both_sums = jnp.einsum(
            "vklp,pvn->vkln", both_weights, value_slice, preferred_element_type=jnp.float32
        )
        running_total = running_total * fade[..., None] + both_sums[:, :group_ratio]
        accum_tangent = (
            accum_tangent * fade[..., None]
            + both_sums[:, group_ratio:]
            + jnp.einsum(
                "vklp,pvn->vkln",
                lower_bound,
                value_slice_gradient,
                preferred_element_type=jnp.float32,
            )
        )
        return (new_high, total, cross, running_total, accum_tangent)

    def attend(totals, query_block_rows, query_rows_gradient, qstart, block_data, first_row):
        row_count = query_block_rows.shape[0]
        qpos = qstart + jnp.arange(row_count, dtype=jnp.int32)
        qdocs = doc_ids[jnp.clip(qpos, 0, whole_len - 1)]
        block_len = block_data.shape[1]
        last_row = jnp.minimum(first_row + block_len - 1, qstart + row_count - 1)
        last_doc = doc_ids[jnp.clip(last_row, 0, whole_len - 1)]
        live = (
            (first_row <= qstart + row_count - 1)
            & (first_row + block_len - 1 >= 0)
            & (last_doc >= qdocs[0])
        )
        return lax.cond(
            live,
            lambda current: update(
                current, query_block_rows, query_rows_gradient, qpos, qdocs, block_data, first_row
            ),
            lambda current: current,
            totals,
        )

    def attend_all(totals, block_data, first_row):
        return attend(totals, query_rows, dquery_rows, query_first, block_data, first_row)

    zero_rows = jnp.zeros((groups, group_ratio, tok_count), jnp.float32)
    zero_accum = jnp.zeros((groups, group_ratio, tok_count, HEAD_DIM), jnp.float32)
    totals = attend_all(
        (
            jnp.full((groups, group_ratio, tok_count), -1e30, jnp.float32),
            zero_rows,
            zero_rows,
            zero_accum,
            zero_accum,
        ),
        packed,
        query_first,
    )
    moving = packed
    for hop_number in range(1, DOC_SHARDS + 1):
        moving = from_behind(moving, "seq", 1)
        totals = attend_all(totals, moving, (shard_index - hop_number) * tok_count)
    highest, total, cross, running_total, accum_tangent = totals
    output = running_total / total[..., None]
    dout = accum_tangent / total[..., None] - (cross / total)[..., None] * output
    dout = (
        dout.transpose(2, 0, 1, 3)
        .reshape(tok_count, groups * group_ratio * HEAD_DIM)
        .astype(jnp.bfloat16)
    )
    partial_out = jnp.dot(dout, out_weight, preferred_element_type=jnp.float32)
    layer_tangent = sent_and_summed(partial_out.astype(jnp.bfloat16), "head", 1).astype(
        jnp.bfloat16
    )
    cot_rows = cotangent[0]
    seq_share = lax.psum_scatter(
        lax.dot_general(
            cot_rows, dout, (((0,), (0,)), ((), ())), preferred_element_type=jnp.float32
        ).astype(jnp.bfloat16),
        "seq",
        scatter_dimension=0,
        tiled=True,
    )
    weight_hvp = sent_and_summed(seq_share, "dp", 0)
    return (layer_tangent[None], weight_hvp)


def solution(mesh):
    placed = (
        P("dp", "seq", "head"),
        P("dp", "seq", "head"),
        P("dp", "seq", "head"),
        P("dp", "seq", "head"),
        P("dp", "seq", "head"),
        P("dp", "seq", "head"),
        P("dp", None),
        P("head", None),
        P("dp", "seq", None),
    )
    return jax.shard_map(
        on_device,
        mesh=mesh,
        in_specs=placed,
        out_specs=(P("dp", "seq", "head"), P(("seq", "dp"), "head")),
        check_vma=False,
    )
```

profile of v0, /device:TPU:1, one launch (start us, length us, event | category | flops | bytes accessed | tf_op | source)
XLA Modules:
  0.0 226.6 jit_solution(4053846902493172352)
XLA Ops:
  7.2 0.0 copy-start
  7.2 0.0 reduce-scatter.2.cloned.1.call-start
  7.2 1.0 copy.114
  8.3 1.0 copy.115
  9.2 1.0 copy.116
  10.2 1.0 copy.117
  11.2 4.6 %collective-permute-start = (bf16[4,128,256]{1,2,0:T(8,128)(2,1)S(1)}, bf16[4,128,256]{1,2,0:T(8,128)(2,1)}, u32[]{:S(2)}, u32[]{:S(2)}) collective-permute-start(bf16[4,128,256]{1,2,0:T(8,128)(2,1)S(1)} %pad_maximum_fusion), channel_id=1, source_target_pairs={{0,16},{16,32},{32,48},{48,64},{64,80},{80,96},{96,112},{112,128},... | collective-permute-start | bytes 786440 | tf_op jit(solution)/shard_map/ppermute | solution.py:15
  15.8 4.3 %collective-permute-done = bf16[4,128,256]{1,2,0:T(8,128)(2,1)} collective-permute-done((bf16[4,128,256]{1,2,0:T(8,128)(2,1)S(1)}, bf16[4,128,256]{1,2,0:T(8,128)(2,1)}, u32[]{:S(2)}, u32[]{:S(2)}) %collective-permute-start) | collective-permute-done | bytes 262176 | tf_op jit(solution)/shard_map/ppermute | solution.py:15
  20.1 4.9 %collective-permute-start.1 = (bf16[4,128,256]{1,2,0:T(8,128)(2,1)}, bf16[4,128,256]{1,2,0:T(8,128)(2,1)}, u32[]{:S(2)}, u32[]{:S(2)}) collective-permute-start(bf16[4,128,256]{1,2,0:T(8,128)(2,1)} %collective-permute-done), channel_id=1, source_target_pairs={{0,16},{16,32},{32,48},{48,64},{64,80},{80,96},{96,112},{112,128},... | collective-permute-start | bytes 786440 | tf_op jit(solution)/shard_map/ppermute | solution.py:15
  25.0 0.7 copy.109
  25.8 0.1 reduce.1
  25.9 0.1 convert_reduce_fusion.1
  26.0 1.1 gather_fusion.3
  27.2 0.7 fusion.64
  28.5 1.1 copy.110
  29.6 1.8 copy.111
  32.7 9.7 %conditional.3 = (f32[2,4,128]{2,1,0:T(4,128)}, f32[2,4,128]{2,1,0:T(4,128)S(1)}, f32[2,4,128]{2,1,0:T(4,128)S(1)}, f32[2,4,128,128]{3,2,1,0:T(8,128)S(1)}, f32[2,4,128,128]{3,2,1,0:T(8,128)S(1)}) conditional(s32[]{:T(128)} %convert_element_type.58, () %tuple.29, (s32[]{:T(128)}, s32[2048]{0:T(1024)S(1)}, s32[128]{0:T(128)S(1)}, s32[128]{0:T(128)S(1)}, ...), branch_computations={%region_2.3_spmd, %region_3.7_spmd} | conditional | flops 204675072 | bytes 10622288 | solution.py:118
  32.8 1.1 gather_fusion
  34.0 0.1 and_and_fusion
  34.1 0.2 copy.112
  34.3 1.1 copy.113
  35.4 0.9 squeeze_stack_squeeze.8
  36.3 0.3 convolution_bitcast_fusion
  36.6 0.1 fusion.11
  36.7 0.6 exponential_multiply_fusion
  37.2 0.9 fusion.12
  38.1 0.9 squeeze_stack_squeeze.9
  39.0 1.0 fusion.59
  40.0 0.9 squeeze_stack_squeeze.10
  40.8 0.3 fusion.7
  41.2 0.3 convolution_add_fusion
  41.5 0.2 slice_add_fusion.1
  41.7 0.7 fusion.21
  42.4 1.2 conditional.5
  42.5 0.2 copy.171
  42.7 1.0 copy.173
  43.7 1.2 subtract_convert_fusion
  44.9 5.6 %convert_bitcast_fusion = bf16[4096,1024]{0,1:T(8,128)(2,1)} fusion(bf16[128,1024]{0,1:T(8,128)(2,1)S(1)} %bitcast.147, bf16[1,128,4096]{2,1,0:T(8,128)(2,1)S(1)} %copy-done), kind=kOutput, calls=%fused_computation.105 | convolution fusion | flops 1077936128 | bytes 9699328 | tf_op jit(solution)/shard_map/dot_general | solution.py:161
  50.4 0.0 reduce-scatter.2.cloned.1.call-update
  50.4 4.7 %convolution_convert_fusion = bf16[128,4096]{1,0:T(8,128)(2,1)S(1)} fusion(bf16[128,1024]{0,1:T(8,128)(2,1)S(1)} %bitcast.148, bf16[1024,4096]{1,0:T(8,128)(2,1)} %param.22), kind=kOutput, calls=%fused_computation.106 | convolution fusion | flops 1074266112 | bytes 9699328 | tf_op jit(solution)/shard_map/dot_general | solution.py:155
  55.1 1.1 copy.187
  56.2 3.6 %all-to-all-start = ((bf16[2,128,2048]{2,1,0:T(8,128)(2,1)}), bf16[2,128,2048]{2,1,0:T(8,128)(2,1)S(1)}, u32[]{:S(2)}, u32[]{:S(2)}) async-start(bf16[2,128,2048]{2,1,0:T(8,128)(2,1)} %bitcast.121), calls=%async_computation | async-start | bytes 2097152 | tf_op jit(solution)/shard_map/all_to_all | solution.py:26
  59.8 141.5 %reduce-scatter.2.cloned.1.call-done = bf16[256,1024]{0,1:T(8,128)(2,1)} async-done(((bf16[4096,1024]{0,1:T(8,128)(2,1)}), bf16[256,1024]{0,1:T(8,128)(2,1)}) %reduce-scatter.2.cloned.1.call-update) | async-done | bytes 524304 | tf_op jit(solution)/shard_map/reduce_scatter | solution.py:160
  201.4 2.0 copy.125
  203.4 6.2 %all-to-all-start.1 = ((bf16[8,32,1024]{2,1,0:T(8,128)(2,1)}), bf16[8,32,1024]{2,1,0:T(8,128)(2,1)S(1)}, u32[]{:S(2)}, u32[]{:S(2)}) async-start(bf16[8,32,1024]{2,1,0:T(8,128)(2,1)} %bitcast.43), calls=%async_computation.2 | async-start | bytes 1048576 | tf_op jit(solution)/shard_map/all_to_all | solution.py:26
  209.6 1.1 reduce_sum.85
  210.8 8.2 %all-to-all-done.1 = bf16[8,32,1024]{2,1,0:T(8,128)(2,1)S(1)} async-done(((bf16[8,32,1024]{2,1,0:T(8,128)(2,1)}), bf16[8,32,1024]{2,1,0:T(8,128)(2,1)S(1)}, u32[]{:S(2)}, u32[]{:S(2)}) %all-to-all-start.1) | async-done | bytes 524320 | tf_op jit(solution)/shard_map/all_to_all | solution.py:26
  219.0 0.7 convert_reduce_fusion
  (17 shorter events, 0.2 us)
Async XLA Ops:
  7.2 37.7 %copy-start = (bf16[1,128,4096]{2,1,0:T(8,128)(2,1)S(1)}, bf16[1,128,4096]{2,1,0:T(8,128)(2,1)}, u32[]{:S(2)}) copy-start(bf16[1,128,4096]{2,1,0:T(8,128)(2,1)} %param.23) | copy-start | bytes 3145732
  7.2 194.2 %reduce-scatter.2.cloned.1.call-start = ((), (), s32[]{:S(2)}) async-start(), calls=%async_computation.3 | async-start | bytes 8912896 | tf_op jit(solution)/shard_map/reduce_scatter | solution.py:160
  11.2 8.9 %collective-permute-start = (bf16[4,128,256]{1,2,0:T(8,128)(2,1)S(1)}, bf16[4,128,256]{1,2,0:T(8,128)(2,1)}, u32[]{:S(2)}, u32[]{:S(2)}) collective-permute-start(bf16[4,128,256]{1,2,0:T(8,128)(2,1)S(1)} %pad_maximum_fusion), channel_id=1, source_target_pairs={{0,16},{16,32},{32,48},{48,64},{64,80},{80,96},{96,112},{112,128},... | collective-permute-start | bytes 786440 | tf_op jit(solution)/shard_map/ppermute | solution.py:15
  20.1 22.3 %collective-permute-start.1 = (bf16[4,128,256]{1,2,0:T(8,128)(2,1)}, bf16[4,128,256]{1,2,0:T(8,128)(2,1)}, u32[]{:S(2)}, u32[]{:S(2)}) collective-permute-start(bf16[4,128,256]{1,2,0:T(8,128)(2,1)} %collective-permute-done), channel_id=1, source_target_pairs={{0,16},{16,32},{32,48},{48,64},{64,80},{80,96},{96,112},{112,128},... | collective-permute-start | bytes 786440 | tf_op jit(solution)/shard_map/ppermute | solution.py:15
  32.7 8.4 %copy-start.1 = (bf16[1,128,256]{2,1,0:T(8,128)(2,1)S(1)}, bf16[1,128,256]{2,1,0:T(8,128)(2,1)}, u32[]{:S(2)}) copy-start(bf16[1,128,256]{2,1,0:T(8,128)(2,1)} %get-tuple-element.95) | copy-start | bytes 196612 | tf_op jit(solution)/shard_map/cond
  56.2 147.2 %all-to-all-start = ((bf16[2,128,2048]{2,1,0:T(8,128)(2,1)}), bf16[2,128,2048]{2,1,0:T(8,128)(2,1)S(1)}, u32[]{:S(2)}, u32[]{:S(2)}) async-start(bf16[2,128,2048]{2,1,0:T(8,128)(2,1)} %bitcast.121), calls=%async_computation | async-start | bytes 2097152 | tf_op jit(solution)/shard_map/all_to_all | solution.py:26
  203.4 15.6 %all-to-all-start.1 = ((bf16[8,32,1024]{2,1,0:T(8,128)(2,1)}), bf16[8,32,1024]{2,1,0:T(8,128)(2,1)S(1)}, u32[]{:S(2)}, u32[]{:S(2)}) async-start(bf16[8,32,1024]{2,1,0:T(8,128)(2,1)} %bitcast.43), calls=%async_computation.2 | async-start | bytes 1048576 | tf_op jit(solution)/shard_map/all_to_all | solution.py:26
Sparse Core Ops, SparseCore 0:
  50.6 150.7 reduce-scatter.1
where the time goes:
time: 231 us; the launch traced here: 227 us
  waiting for transfers between devices  154 us (67%)
  starting transfers between devices  19.4 us (8%)
  local copies, waits for them, and re-layouts  18.8 us (8%)
  between operations  16.1 us (7%)
  matrix products  12.2 us (5%)
  other arithmetic  5.92 us (3%)
    reduce_scatter x1, waiting for transfers between devices, on_device(): lax.psum_scatter(lax.dot_general(cot_rows, dout, (((0,), (0,)), ((), ()))...  142 us
    all_to_all x2, starting transfers between devices, sent_and_summed(): lax.all_to_all(in_blocks(array, dim, length), axis, 0, 0, tiled=True)  9.82 us
    ppermute x2, starting transfers between devices, from_behind(): return lax.ppermute(block, axis, route)  9.54 us
    all_to_all x2, waiting for transfers between devices, sent_and_summed(): lax.all_to_all(in_blocks(array, dim, length), axis, 0, 0, tiled=True)  8.24 us
    unnamed x8, local copies, waits for them, and re-layouts  6.83 us
    dot_general x1, matrix products, on_device(): lax.dot_general(cot_rows, dout, (((0,), (0,)), ((), ())), preferred_eleme...  5.55 us
    dot_general x1, matrix products, on_device(): partial_out = jnp.dot(dout, out_weight, preferred_element_type=jnp.float32)  4.67 us
  transfers between devices with their start and end apart: 5, of which 3 were waited for; matrix products, arithmetic and copies ran while one was open for 11% of the time, Pallas kernels for 0%

commit v1 on v0

v1 whole, which is shorter than its diff:
```python
import jax
import jax.numpy as jnp
from jax import lax
from jax.experimental import pallas as pl
from jax.experimental.pallas import tpu as pltpu
from jax.sharding import PartitionSpec as P

HEAD_DIM = 128
TOK = 128
GROUPS = 2
RATIO = 4
NX = 4
NZ = 4
DP = 8
DOCS = 17
COLS = RATIO * HEAD_DIM
SLICE = 512
BF16 = jnp.bfloat16
F32 = jnp.float32
MESH = pl.DeviceIdType.MESH


def kernel(
    len_ref, q_hbm, k_hbm, v_hbm, dq_hbm, dk_hbm, dv_hbm, w_hbm, cot_hbm,
    lt_ref, hvp_ref,
    cot_v, cot_send, cot_all, dout, kv, relay, q_v, dq_v, w_v,
    part, part_in, sums, z_send, z_in, lt_send, lt_own, lt_in,
    load_sem, kv_load, z_s, z_r, x1_s, x1_r, x2_s, x2_r,
    cot_s, cot_r, own_sem, y_s, y_r, p_s, p_r, f_s, f_r,
    px_s, px_r, pz_s, pz_r, lt_s, lt_r,
):
    seq = lax.axis_index("seq")
    dp = lax.axis_index("dp")
    head = lax.axis_index("head")
    x = lax.rem(seq, NX)
    z = lax.div(seq, NX)
    core = lax.rem(dp, 2)

    def x_dev(k):
        return {"seq": z * NX + lax.rem(x + k, NX)}

    def z_dev(k):
        return {"seq": lax.rem(z + k, NZ) * NX + x}

    def d_at(k):
        return lax.rem(dp + k, DP)

    partner = dp + 1 - 2 * core

    def remote(src, dst, send, recv, device):
        return pltpu.make_async_remote_copy(
            src_ref=src, dst_ref=dst, send_sem=send, recv_sem=recv,
            device_id=device, device_id_type=MESH,
        )

    barrier = pltpu.get_barrier_semaphore()
    peers = [x_dev(k) for k in range(1, NX)] + [z_dev(k) for k in range(1, NZ)]
    peers += [{"dp": d_at(k)} for k in range(1, DP)] + [{"head": 1 - head}]
    for peer in peers:
        pl.semaphore_signal(barrier, inc=1, device_id=peer, device_id_type=MESH)

    loads = [
        pltpu.make_async_copy(src, dst, load_sem.at[i])
        for i, (src, dst) in enumerate(
            [(cot_hbm.at[0], cot_v), (q_hbm.at[0], q_v), (dq_hbm.at[0], dq_v), (w_hbm, w_v)]
        )
    ]
    cot_load, q_load, dq_load, w_load = loads
    cot_load.start()
    tensors = (k_hbm, dk_hbm, v_hbm, dv_hbm)

    def own(g, a):
        return tensors[a].at[0, :, pl.ds(g * HEAD_DIM, HEAD_DIM)]

    pieces = [(g, a) for g in range(GROUPS) for a in range(4)]
    kv_loads = {
        p: pltpu.make_async_copy(own(*p), kv.at[p[0], p[1], 2], kv_load.at[p[0], p[1]])
        for p in pieces
    }
    for p in pieces:
        kv_loads[p].start()
    q_load.start()
    dq_load.start()
    w_load.start()

    cot_load.wait()

    @pl.loop(0, NX * NZ)
    def _(s):
        first = pl.multiple_of(s * 256, 256)
        turned = cot_v[:, pl.ds(first, 256)].T
        row = pl.multiple_of((lax.rem(s, NX) * NZ + lax.div(s, NX)) * 32, 32)
        for d in range(DP):
            cot_send[d, pl.ds(row, 32), :] = turned[d * 32 : (d + 1) * 32]

    pl.semaphore_wait(barrier, len(peers))

    to_z = {
        p: remote(own(*p), relay.at[p[0], p[1]], z_s.at[p[0], p[1]], z_r.at[p[0], p[1]], z_dev(1))
        for p in pieces
    }

    def to_x(p, k, src):
        g, a = p
        send, recv = ((x1_s, x1_r), (x2_s, x2_r))[k - 1]
        return remote(src, kv.at[g, a, 2 - k], send.at[g, a], recv.at[g, a], x_dev(k))

    for p in pieces:
        @pl.when(x >= 2)
        def _():
            to_z[p].start()

        @pl.when(x < 3)
        def _():
            to_x(p, 1, own(*p)).start()

        @pl.when(x < 2)
        def _():
            to_x(p, 2, own(*p)).start()

    cot_copies = [
        remote(cot_send.at[d_at(k)], cot_all.at[dp], cot_s.at[k - 1], cot_r.at[k - 1], {"dp": d_at(k)})
        for k in range(1, DP)
    ]
    for copy in cot_copies:
        copy.start()
    cot_own = pltpu.make_async_copy(cot_send.at[dp], cot_all.at[dp], own_sem)
    cot_own.start()

    for p in pieces:
        @pl.when(x >= 2)
        def _():
            to_z[p].wait_recv()
            to_x(p, 2, relay.at[p[0], p[1]]).start()

        @pl.when(x == 3)
        def _():
            to_x(p, 1, relay.at[p[0], p[1]]).start()

    base = seq * TOK
    query_pos = lax.broadcasted_iota(jnp.int32, (TOK, 1), 0) + base
    start = jnp.zeros((TOK, 1), jnp.int32)
    end = jnp.int32(0)
    for i in range(DOCS):
        end = end + len_ref[0, i]
        start = jnp.where(query_pos >= end, jnp.maximum(start, end), start)
    key_pos = lax.broadcasted_iota(jnp.int32, (TOK, 3 * TOK), 1) + (base - 2 * TOK)
    allowed = ((key_pos >= start) & (key_pos <= query_pos))[None]

    q_load.wait()
    dq_load.wait()
    scale = HEAD_DIM ** (-0.5)
    nt = (((1,), (1,)), ((), ()))
    y_copies, p_copies = {}, {}
    for g in range(GROUPS):
        for a in range(4):
            kv_loads[g, a].wait()
            to_x((g, a), 1, relay.at[g, a]).wait_recv()
            to_x((g, a), 2, relay.at[g, a]).wait_recv()
        heads = [slice((g * RATIO + r) * HEAD_DIM, (g * RATIO + r + 1) * HEAD_DIM) for r in range(RATIO)]
        q = jnp.concatenate([q_v[:, h] for h in heads], axis=0)
        dq = jnp.concatenate([dq_v[:, h] for h in heads], axis=0)
        key, dkey, value, dvalue = (kv[g, a].reshape(3 * TOK, HEAD_DIM) for a in range(4))
        scores = lax.dot_general(q, key, nt, preferred_element_type=F32)
        tangent = lax.dot_general(
            jnp.concatenate([dq, q], axis=1), jnp.concatenate([key, dkey], axis=1), nt,
            preferred_element_type=F32,
        )
        scores = jnp.where(allowed, scores.reshape(RATIO, TOK, 3 * TOK) * scale, -1e30)
        high = jnp.max(scores, axis=-1, keepdims=True)
        weight = jnp.where(allowed, jnp.exp(scores - high), 0.0)
        weighted = weight * (tangent.reshape(RATIO, TOK, 3 * TOK) * scale)
        total = jnp.sum(weight, axis=-1, keepdims=True).reshape(RATIO * TOK, 1)
        cross = jnp.sum(weighted, axis=-1, keepdims=True).reshape(RATIO * TOK, 1)
        low = weight.astype(BF16).reshape(RATIO * TOK, 3 * TOK)
        low_tangent = weighted.astype(BF16).reshape(RATIO * TOK, 3 * TOK)
        both = jnp.dot(low, jnp.concatenate([value, dvalue], axis=1), preferred_element_type=F32)
        accum = both[:, :HEAD_DIM]
        accum_tangent = both[:, HEAD_DIM:] + jnp.dot(low_tangent, value, preferred_element_type=F32)
        inverse = 1.0 / total
        result = ((accum_tangent - (cross * inverse) * accum) * inverse).astype(BF16)
        for r in range(RATIO):
            dout[g, dp, :, r * HEAD_DIM : (r + 1) * HEAD_DIM] = result[r * TOK : (r + 1) * TOK]
        for k in range(1, 4):
            y_copies[g, k] = remote(
                dout.at[g, dp], dout.at[g, dp], y_s.at[g, k - 1], y_r.at[g, k - 1], {"dp": d_at(2 * k)}
            )
            y_copies[g, k].start()
        p_copies[g] = remote(dout.at[g, dp], dout.at[g, dp], p_s.at[g], p_r.at[g], {"dp": partner})
        p_copies[g].start()

    w_load.wait()
    rows = jnp.concatenate([dout[g, dp] for g in range(GROUPS)], axis=1)
    lt_copies = []
    for j in range(4):
        first = pl.multiple_of((1 - head) * 2048 + j * 512, 512)
        lt_send[j] = jnp.dot(rows, w_v[:, pl.ds(first, 512)], preferred_element_type=F32).astype(BF16)
        copy = remote(lt_send.at[j], lt_in.at[j], lt_s.at[j], lt_r.at[j], {"head": 1 - head})
        copy.start()
        lt_copies.append(copy)
    for j in range(4):
        first = pl.multiple_of(head * 2048 + j * 512, 512)
        lt_own[j] = jnp.dot(rows, w_v[:, pl.ds(first, 512)], preferred_element_type=F32)

    cot_own.wait()
    for copy in cot_copies:
        copy.wait_recv()
    f_copies, px_copies, pz_copies = {}, {}, {}
    for g in range(GROUPS):
        for k in range(1, 4):
            y_copies[g, k].wait_recv()
            source = d_at(DP - 2 * k)
            f_copies[g, k] = remote(
                dout.at[g, source], dout.at[g, source], f_s.at[g, k - 1], f_r.at[g, k - 1], {"dp": partner}
            )
            f_copies[g, k].start()
    for g in range(GROUPS):
        p_copies[g].wait_recv()
        for k in range(1, 4):
            f_copies[g, k].wait_recv()
        left = jnp.concatenate([cot_all[d] for d in range(DP)], axis=1)
        terms = jnp.dot(left, dout[g].reshape(DP * TOK, COLS), preferred_element_type=F32)
        for t in range(NX):
            part[g, t] = terms[t * 128 : (t + 1) * 128].astype(BF16)
        for k in range(1, NX):
            px_copies[g, k] = remote(
                part.at[g, lax.rem(x + k, NX)], part_in.at[g, k - 1],
                px_s.at[g, k - 1], px_r.at[g, k - 1], x_dev(k),
            )
            px_copies[g, k].start()

    for g in range(GROUPS):
        acc = part[g, x].astype(F32)
        for k in range(1, NX):
            px_copies[g, k].wait_recv()
            acc = acc + part_in[g, k - 1].astype(F32)
        sums[g] = acc.reshape(NZ, 32, COLS)
        z_send[g] = acc.astype(BF16).reshape(NZ, 32, COLS)
        for k in range(1, NZ):
            pz_copies[g, k] = remote(
                z_send.at[g, lax.rem(z + k, NZ)], z_in.at[g, k - 1],
                pz_s.at[g, k - 1], pz_r.at[g, k - 1], z_dev(k),
            )
            pz_copies[g, k].start()

    for j in range(4):
        lt_copies[j].wait_recv()
        lt_ref[0, :, j * 512 : (j + 1) * 512] = (lt_own[j] + lt_in[j].astype(F32)).astype(BF16)

    for g in range(GROUPS):
        acc = sums[g, z]
        for k in range(1, NZ):
            pz_copies[g, k].wait_recv()
            acc = acc + z_in[g, k - 1].astype(F32)
        hvp_ref[:, g * COLS : (g + 1) * COLS] = acc

    for p in pieces:
        @pl.when(x >= 2)
        def _():
            to_z[p].wait_send()

        for k in (1, 2):
            to_x(p, k, relay.at[p[0], p[1]]).wait_send()
    for copies in (y_copies, p_copies, f_copies, px_copies, pz_copies):
        for copy in copies.values():
            copy.wait_send()
    for copy in cot_copies + lt_copies:
        copy.wait_send()


def on_device(*args):
    lengths, others = args[6], args[:6] + args[7:]
    dma = pltpu.SemaphoreType.DMA
    vmem = pltpu.VMEM
    return pl.pallas_call(
        kernel,
        name="tangent",
        out_shape=(
            jax.ShapeDtypeStruct((1, TOK, 2048), BF16),
            jax.ShapeDtypeStruct((32, 1024), F32),
        ),
        in_specs=[pl.BlockSpec(memory_space=pltpu.SMEM)] + [pl.BlockSpec(memory_space=pl.ANY)] * 8,
        out_specs=(pl.BlockSpec(memory_space=vmem), pl.BlockSpec(memory_space=vmem)),
        scratch_shapes=[
            vmem((TOK, 4096), BF16),
            vmem((DP, SLICE, TOK), BF16),
            vmem((DP, SLICE, TOK), BF16),
            vmem((GROUPS, DP, TOK, COLS), BF16),
            vmem((GROUPS, 4, 3, TOK, HEAD_DIM), BF16),
            vmem((GROUPS, 4, TOK, HEAD_DIM), BF16),
            vmem((TOK, 1024), BF16),
            vmem((TOK, 1024), BF16),
            vmem((1024, 4096), BF16),
            vmem((GROUPS, NX, 128, COLS), BF16),
            vmem((GROUPS, NX - 1, 128, COLS), BF16),
            vmem((GROUPS, NZ, 32, COLS), F32),
            vmem((GROUPS, NZ, 32, COLS), BF16),
            vmem((GROUPS, NZ - 1, 32, COLS), BF16),
            vmem((4, TOK, 512), BF16),
            vmem((4, TOK, 512), F32),
            vmem((4, TOK, 512), BF16),
            dma((4,)),
            dma((GROUPS, 4)),
            dma((GROUPS, 4)),
            dma((GROUPS, 4)),
            dma((GROUPS, 4)),
            dma((GROUPS, 4)),
            dma((GROUPS, 4)),
            dma((GROUPS, 4)),
            dma((DP - 1,)),
            dma((DP - 1,)),
            dma,
            dma((GROUPS, 3)),
            dma((GROUPS, 3)),
            dma((GROUPS,)),
            dma((GROUPS,)),
            dma((GROUPS, 3)),
            dma((GROUPS, 3)),
            dma((GROUPS, NX - 1)),
            dma((GROUPS, NX - 1)),
            dma((GROUPS, NZ - 1)),
            dma((GROUPS, NZ - 1)),
            dma((4,)),
            dma((4,)),
        ],
        compiler_params=pltpu.CompilerParams(
            collective_id=0, has_side_effects=True, vmem_limit_bytes=60 * 1024 * 1024
        ),
    )(lengths, *others)


def solution(mesh):
    placed = (
        P("dp", "seq", "head"),
        P("dp", "seq", "head"),
        P("dp", "seq", "head"),
        P("dp", "seq", "head"),
        P("dp", "seq", "head"),
        P("dp", "seq", "head"),
        P("dp", None),
        P("head", None),
        P("dp", "seq", None),
    )
    return jax.shard_map(
        on_device,
        mesh=mesh,
        in_specs=placed,
        out_specs=(P("dp", "seq", "head"), P(("seq", "dp"), "head")),
        check_vma=False,
    )
```

time: 231 us -> 63.1 us (0.27)
  the two profiles are of different devices: /device:TPU:1 before, /device:TPU:4 now
where the time goes in v1:
time: 63.1 us; the launch traced here: 62.9 us
  Pallas kernels  58.8 us (93%)
  local copies, waits for them, and re-layouts  3.45 us (5%)
  between operations  0.64 us (1%)
    pallas_call x1, Pallas kernels, on_device(): pl.pallas_call(kernel, name='tangent', out_shape=(jax.ShapeDtypeStruct((1...  58.8 us
    unnamed x2, local copies, waits for them, and re-layouts  3.45 us

profile of v1, /device:TPU:4, one launch (start us, length us, event | category | flops | bytes accessed | tf_op | source)
XLA Modules:
  0.0 62.9 jit_solution(11586405191319989953)
XLA Ops:
  0.6 58.8 %tangent.1 = (bf16[1,128,2048]{2,1,0:T(8,128)(2,1)}, f32[32,1024]{1,0:T(8,128)}) custom-call(s32[1,17]{1,0:T(1,128)} %len_ref.1, bf16[1,128,1024]{2,1,0:T(8,128)(2,1)} %q_hbm.1, bf16[1,128,256]{2,1,0:T(8,128)(2,1)} %k_hbm.1, bf16[1,128,256]{2,1,0:T(8,128)(2,1)} %v_hbm.1, bf16[1,128,1024]{2,1,0:T(8,128)(2,1)} %dq_hbm.1, bf16[1,128,256]{2,1,0:T(8,128)(2,1)} %dk_hbm.1, ...), custom_call_target="tpu_custom_call" | custom-call | tf_op jit(solution)/shard_map/tangent/pallas_call | solution.py:275
  59.5 1.9 %copy.13 = bf16[1,128,2048]{2,1,0:T(8,128)(2,1)} copy(bf16[1,128,2048]{2,1,0:T(8,128)(2,1)} %get-tuple-element.4) | data formatting | bytes 1048576
  61.4 1.6 %copy.14 = f32[32,1024]{1,0:T(8,128)} copy(f32[32,1024]{1,0:T(8,128)} %get-tuple-element.5) | data formatting | bytes 262144

commit v2 on v1

v2 whole, which is shorter than its diff:
```python
import jax
import jax.numpy as jnp
from jax import lax
from jax.experimental import pallas as pl
from jax.experimental.pallas import tpu as pltpu
from jax.sharding import PartitionSpec as P

HEAD_DIM = 128
TOK = 128
GROUPS = 2
RATIO = 4
NX = 4
NZ = 4
DP = 8
DOCS = 17
CHUNKS = 4
WIDTH = 256
SLICE = 512
BF16 = jnp.bfloat16
F32 = jnp.float32
MESH = pl.DeviceIdType.MESH


def kernel(
    len_ref, q_hbm, k_hbm, v_hbm, dq_hbm, dk_hbm, dv_hbm, w_hbm, cot_hbm,
    lt_ref, hvp_ref,
    cot_v, cot_send, cot_all, dout, kv, early, q_v, dq_v, w_v,
    part, part_in, sums, z_send, z_in, lt_send, lt_own, lt_in,
    load_sem, kv_load, near_s, near_r, far_s, far_r, side_s, cross_s, early_r,
    cot_s, cot_r, own_sem, y_s, y_r, pair_s, pair_r,
    px_s, px_r, pz_s, pz_r, lt_s, lt_r,
):
    seq = lax.axis_index("seq")
    dp = lax.axis_index("dp")
    head = lax.axis_index("head")
    x = lax.rem(seq, NX)
    z = lax.div(seq, NX)
    core = lax.rem(dp, 2)

    def x_dev(k):
        return {"seq": z * NX + lax.rem(x + k, NX)}

    def z_dev(k):
        return {"seq": lax.rem(z + k, NZ) * NX + x}

    def seq_dev(k):
        return {"seq": lax.rem(seq + k, NX * NZ)}

    def d_at(k):
        return lax.rem(dp + k, DP)

    partner = dp + 1 - 2 * core

    def remote(src, dst, send, recv, device):
        return pltpu.make_async_remote_copy(
            src_ref=src, dst_ref=dst, send_sem=send, recv_sem=recv,
            device_id=device, device_id_type=MESH,
        )

    barrier = pltpu.get_barrier_semaphore()
    peers = [x_dev(k) for k in range(1, NX)] + [z_dev(k) for k in range(1, NZ)]
    peers += [seq_dev(k) for k in (1, 2, 3, 13, 14, 15)]
    peers += [{"dp": d_at(k)} for k in range(1, DP)] + [{"head": 1 - head}]
    for peer in peers:
        pl.semaphore_signal(barrier, inc=1, device_id=peer, device_id_type=MESH)

    loads = [
        pltpu.make_async_copy(src, dst, load_sem.at[i])
        for i, (src, dst) in enumerate(
            [(cot_hbm.at[0], cot_v), (q_hbm.at[0], q_v), (dq_hbm.at[0], dq_v), (w_hbm, w_v)]
        )
    ]
    cot_load, q_load, dq_load, w_load = loads
    cot_load.start()
    tensors = (k_hbm, dk_hbm, v_hbm, dv_hbm)

    def own(g, a):
        return tensors[a].at[0, :, pl.ds(g * HEAD_DIM, HEAD_DIM)]

    pieces = [(g, a) for g in range(GROUPS) for a in range(4)]
    kv_loads = {
        p: pltpu.make_async_copy(own(*p), kv.at[p[0], p[1], 2], kv_load.at[p[0], p[1]])
        for p in pieces
    }
    for p in pieces:
        kv_loads[p].start()
    q_load.start()
    dq_load.start()

    def turn(first_step, last_step):
        @pl.loop(first_step, last_step)
        def _(s):
            first = pl.multiple_of(s * 256, 256)
            turned = cot_v[:, pl.ds(first, 256)].T
            row = pl.multiple_of((lax.rem(s, NX) * NZ + lax.div(s, NX)) * 32, 32)
            for d in range(DP):
                cot_send[d, pl.ds(row, 32), :] = turned[d * 32 : (d + 1) * 32]

    cot_load.wait()
    turn(0, 8)
    pl.semaphore_wait(barrier, len(peers))

    def near(g, a):
        return remote(own(g, a), kv.at[g, a, 1], near_s.at[g, a], near_r.at[g, a], seq_dev(1))

    def far(g, a):
        return remote(own(g, a), kv.at[g, a, 0], far_s.at[g, a], far_r.at[g, a], seq_dev(2))

    def onward(g, a):
        return remote(kv.at[g, a, 1], kv.at[g, a, 0], side_s.at[g, a], far_r.at[g, a], x_dev(1))

    def ahead(a, k, send):
        return remote(own(1, a), early.at[a], send.at[1, a], early_r.at[1, a], x_dev(k))

    def across_near(a):
        return remote(early.at[a], kv.at[1, a, 1], cross_s.at[1, a], near_r.at[1, a], z_dev(1))

    def across_far(a):
        return remote(early.at[a], kv.at[1, a, 0], cross_s.at[1, a], far_r.at[1, a], seq_dev(3))

    for a in range(4):
        @pl.when(x == 2)
        def _():
            far(0, a).start()

        near(0, a).start()

        @pl.when(x < 2)
        def _():
            far(0, a).start()

    for a in range(4):
        @pl.when(x == 3)
        def _():
            ahead(a, 1, near_s).start()

        @pl.when(x == 2)
        def _():
            ahead(a, 3, far_s).start()

        @pl.when(x < 3)
        def _():
            near(1, a).start()

    turn(8, 16)
    w_load.start()

    cot_copies = [
        remote(cot_send.at[d_at(k)], cot_all.at[dp], cot_s.at[k - 1], cot_r.at[k - 1], {"dp": d_at(k)})
        for k in range(1, DP)
    ]
    for copy in cot_copies:
        copy.start()
    cot_own = pltpu.make_async_copy(cot_send.at[dp], cot_all.at[dp], own_sem)
    cot_own.start()

    for a in range(4):
        @pl.when(x == 0)
        def _():
            ahead(a, 1, near_s).wait_recv()
            across_near(a).start()

        @pl.when(x == 1)
        def _():
            ahead(a, 3, far_s).wait_recv()
            across_far(a).start()

    base = seq * TOK
    query_pos = lax.broadcasted_iota(jnp.int32, (TOK, 1), 0) + base
    start = jnp.zeros((TOK, 1), jnp.int32)
    end = jnp.int32(0)
    for i in range(DOCS):
        end = end + len_ref[0, i]
        start = jnp.where(query_pos >= end, jnp.maximum(start, end), start)
    key_pos = lax.broadcasted_iota(jnp.int32, (TOK, 3 * TOK), 1) + (base - 2 * TOK)
    allowed = ((key_pos >= start) & (key_pos <= query_pos))[None]

    q_load.wait()
    dq_load.wait()
    scale = HEAD_DIM ** (-0.5)
    nt = (((1,), (1,)), ((), ()))
    y_copies, pair_copies = {}, {}

    def pair(c, k):
        ref = dout.at[c, d_at(DP - 2 * k)]
        pair_copies[c, k] = remote(ref, ref, pair_s.at[c, k], pair_r.at[c, k], {"dp": partner})
        pair_copies[c, k].start()

    for g in range(GROUPS):
        for a in range(4):
            near(g, a).wait_recv()

            @pl.when(x == 0)
            def _():
                onward(g, a).start()

        if g == 0:
            @pl.when(x < 2)
            def _():
                for a in range(4):
                    far(1, a).start()

        for a in range(4):
            kv_loads[g, a].wait()
            far(g, a).wait_recv()
        heads = [slice((g * RATIO + r) * HEAD_DIM, (g * RATIO + r + 1) * HEAD_DIM) for r in range(RATIO)]
        q = jnp.concatenate([q_v[:, h] for h in heads], axis=0)
        dq = jnp.concatenate([dq_v[:, h] for h in heads], axis=0)
        key, dkey, value, dvalue = (kv[g, a].reshape(3 * TOK, HEAD_DIM) for a in range(4))
        scores = lax.dot_general(q, key, nt, preferred_element_type=F32)
        tangent = lax.dot_general(
            jnp.concatenate([dq, q], axis=1), jnp.concatenate([key, dkey], axis=1), nt,
            preferred_element_type=F32,
        )
        scores = jnp.where(allowed, scores.reshape(RATIO, TOK, 3 * TOK) * scale, -1e30)
        high = jnp.max(scores, axis=-1, keepdims=True)
        weight = jnp.where(allowed, jnp.exp(scores - high), 0.0)
        weighted = weight * (tangent.reshape(RATIO, TOK, 3 * TOK) * scale)
        total = jnp.sum(weight, axis=-1, keepdims=True).reshape(RATIO * TOK, 1)
        cross = jnp.sum(weighted, axis=-1, keepdims=True).reshape(RATIO * TOK, 1)
        low = weight.astype(BF16).reshape(RATIO * TOK, 3 * TOK)
        low_tangent = weighted.astype(BF16).reshape(RATIO * TOK, 3 * TOK)
        both = jnp.dot(low, jnp.concatenate([value, dvalue], axis=1), preferred_element_type=F32)
        accum = both[:, :HEAD_DIM]
        accum_tangent = both[:, HEAD_DIM:] + jnp.dot(low_tangent, value, preferred_element_type=F32)
        inverse = 1.0 / total
        result = ((accum_tangent - (cross * inverse) * accum) * inverse).astype(BF16)
        for r in range(RATIO):
            h = g * RATIO + r
            column = (h % 2) * HEAD_DIM
            dout[h // 2, dp, :, column : column + HEAD_DIM] = result[r * TOK : (r + 1) * TOK]
        for c in (2 * g, 2 * g + 1):
            mine = dout.at[c, dp]
            for k in (2, 1, 3):
                y_copies[c, k] = remote(
                    mine, mine, y_s.at[c, k - 1], y_r.at[c, k - 1], {"dp": d_at(2 * k)}
                )
                y_copies[c, k].start()
            pair(c, 0)

    w_load.wait()
    rows = jnp.concatenate([dout[c, dp] for c in range(CHUNKS)], axis=1)
    lt_copies, px_copies, pz_copies = [], {}, {}

    def projected(side, j):
        first = pl.multiple_of(side * 2048 + j * 512, 512)
        return jnp.dot(rows, w_v[:, pl.ds(first, 512)], preferred_element_type=F32)

    def project_away(j):
        lt_send[j] = projected(1 - head, j).astype(BF16)
        copy = remote(lt_send.at[j], lt_in.at[j], lt_s.at[j], lt_r.at[j], {"head": 1 - head})
        copy.start()
        lt_copies.append(copy)

    def gather(c):
        for k in (1, 3, 2):
            y_copies[c, k].wait_recv()
            pair(c, k)

    def multiply(c):
        for k in range(4):
            pair_copies[c, k].wait_recv()
        left = jnp.concatenate([cot_all[d] for d in range(DP)], axis=1)
        terms = jnp.dot(left, dout[c].reshape(DP * TOK, WIDTH), preferred_element_type=F32)
        for t in range(NX):
            part[c, t] = terms[t * 128 : (t + 1) * 128].astype(BF16)
        for k in range(1, NX):
            px_copies[c, k] = remote(
                part.at[c, lax.rem(x + k, NX)], part_in.at[c, k - 1],
                px_s.at[c, k - 1], px_r.at[c, k - 1], x_dev(k),
            )
            px_copies[c, k].start()

    def sum_x(c):
        acc = part[c, x].astype(F32)
        for k in range(1, NX):
            px_copies[c, k].wait_recv()
            acc = acc + part_in[c, k - 1].astype(F32)
        sums[c] = acc.reshape(NZ, 32, WIDTH)
        z_send[c] = acc.astype(BF16).reshape(NZ, 32, WIDTH)
        for k in range(1, NZ):
            pz_copies[c, k] = remote(
                z_send.at[c, lax.rem(z + k, NZ)], z_in.at[c, k - 1],
                pz_s.at[c, k - 1], pz_r.at[c, k - 1], z_dev(k),
            )
            pz_copies[c, k].start()

    for j in range(4):
        project_away(j)
    gather(0)
    gather(1)
    cot_own.wait()
    for copy in cot_copies:
        copy.wait_recv()
    multiply(0)
    gather(2)
    multiply(1)
    gather(3)
    multiply(2)
    sum_x(0)
    multiply(3)
    sum_x(1)
    for j in range(4):
        lt_own[j] = projected(head, j)
    sum_x(2)
    sum_x(3)

    for j in range(4):
        lt_copies[j].wait_recv()
        lt_ref[0, :, j * 512 : (j + 1) * 512] = (lt_own[j] + lt_in[j].astype(F32)).astype(BF16)

    for c in range(CHUNKS):
        acc = sums[c, z]
        for k in range(1, NZ):
            pz_copies[c, k].wait_recv()
            acc = acc + z_in[c, k - 1].astype(F32)
        hvp_ref[:, c * WIDTH : (c + 1) * WIDTH] = acc

    for g, a in pieces:
        near(g, a).wait_send()

        @pl.when(x < 3)
        def _():
            far(g, a).wait_send()

        @pl.when(x == 0)
        def _():
            onward(g, a).wait_send()

    for a in range(4):
        @pl.when(x < 2)
        def _():
            across_near(a).wait_send()

    for copies in (y_copies, pair_copies, px_copies, pz_copies):
        for copy in copies.values():
            copy.wait_send()
    for copy in cot_copies + lt_copies:
        copy.wait_send()


def on_device(*args):
    lengths, others = args[6], args[:6] + args[7:]
    dma = pltpu.SemaphoreType.DMA
    vmem = pltpu.VMEM
    return pl.pallas_call(
        kernel,
        name="tangent",
        out_shape=(
            jax.ShapeDtypeStruct((1, TOK, 2048), BF16),
            jax.ShapeDtypeStruct((32, 1024), F32),
        ),
        in_specs=[pl.BlockSpec(memory_space=pltpu.SMEM)] + [pl.BlockSpec(memory_space=pl.ANY)] * 8,
        out_specs=(pl.BlockSpec(memory_space=vmem), pl.BlockSpec(memory_space=vmem)),
        scratch_shapes=[
            vmem((TOK, 4096), BF16),
            vmem((DP, SLICE, TOK), BF16),
            vmem((DP, SLICE, TOK), BF16),
            vmem((CHUNKS, DP, TOK, WIDTH), BF16),
            vmem((GROUPS, 4, 3, TOK, HEAD_DIM), BF16),
            vmem((4, TOK, HEAD_DIM), BF16),
            vmem((TOK, 1024), BF16),
            vmem((TOK, 1024), BF16),
            vmem((1024, 4096), BF16),
            vmem((CHUNKS, NX, 128, WIDTH), BF16),
            vmem((CHUNKS, NX - 1, 128, WIDTH), BF16),
            vmem((CHUNKS, NZ, 32, WIDTH), F32),
            vmem((CHUNKS, NZ, 32, WIDTH), BF16),
            vmem((CHUNKS, NZ - 1, 32, WIDTH), BF16),
            vmem((4, TOK, 512), BF16),
            vmem((4, TOK, 512), F32),
            vmem((4, TOK, 512), BF16),
            dma((4,)),
            *[dma((GROUPS, 4))] * 8,
            dma((DP - 1,)),
            dma((DP - 1,)),
            dma,
            *[dma((CHUNKS, 3))] * 2,
            *[dma((CHUNKS, 4))] * 2,
            *[dma((CHUNKS, 3))] * 4,
            dma((4,)),
            dma((4,)),
        ],
        compiler_params=pltpu.CompilerParams(
            collective_id=0, has_side_effects=True, vmem_limit_bytes=60 * 1024 * 1024
        ),
    )(lengths, *others)


def solution(mesh):
    placed = (
        P("dp", "seq", "head"),
        P("dp", "seq", "head"),
        P("dp", "seq", "head"),
        P("dp", "seq", "head"),
        P("dp", "seq", "head"),
        P("dp", "seq", "head"),
        P("dp", None),
        P("head", None),
        P("dp", "seq", None),
    )
    return jax.shard_map(
        on_device,
        mesh=mesh,
        in_specs=placed,
        out_specs=(P("dp", "seq", "head"), P(("seq", "dp"), "head")),
        check_vma=False,
    )
```

time: 63.1 us -> 59.6 us (0.945)
  the two profiles are of different devices: /device:TPU:4 before, /device:TPU:1 now
where the time goes in v2:
time: 59.6 us; the launch traced here: 59.4 us
  Pallas kernels  55.3 us (93%)
  local copies, waits for them, and re-layouts  3.45 us (6%)
  between operations  0.64 us (1%)
    pallas_call x1, Pallas kernels, on_device(): pl.pallas_call(kernel, name='tangent', out_shape=(jax.ShapeDtypeStruct((1...  55.3 us
    unnamed x2, local copies, waits for them, and re-layouts  3.45 us

profile of v2, /device:TPU:1, one launch (start us, length us, event | category | flops | bytes accessed | tf_op | source)
XLA Modules:
  0.0 59.4 jit_solution(4672004975911917857)
XLA Ops:
  0.6 55.3 %tangent.1 = (bf16[1,128,2048]{2,1,0:T(8,128)(2,1)}, f32[32,1024]{1,0:T(8,128)}) custom-call(s32[1,17]{1,0:T(1,128)} %len_ref.1, bf16[1,128,1024]{2,1,0:T(8,128)(2,1)} %q_hbm.1, bf16[1,128,256]{2,1,0:T(8,128)(2,1)} %k_hbm.1, bf16[1,128,256]{2,1,0:T(8,128)(2,1)} %v_hbm.1, bf16[1,128,1024]{2,1,0:T(8,128)(2,1)} %dq_hbm.1, bf16[1,128,256]{2,1,0:T(8,128)(2,1)} %dk_hbm.1, ...), custom_call_target="tpu_custom_call" | custom-call | tf_op jit(solution)/shard_map/tangent/pallas_call | solution.py:346
  55.9 1.9 %copy.13 = bf16[1,128,2048]{2,1,0:T(8,128)(2,1)} copy(bf16[1,128,2048]{2,1,0:T(8,128)(2,1)} %get-tuple-element.4) | data formatting | bytes 1048576
  57.8 1.6 %copy.14 = f32[32,1024]{1,0:T(8,128)} copy(f32[32,1024]{1,0:T(8,128)} %get-tuple-element.5) | data formatting | bytes 262144

commit v3 on v2

--- a/solution.py
+++ b/solution.py
@@ -339,17 +339,35 @@
         copy.wait_send()
 
 
+def hand_over(lt_in, hvp_in, lt_out, hvp_out, lt_v, hvp_v, in_sem, out_sem):
+    steps = []
+    for i in range(4):
+        rows = pl.ds(i * 32, 32)
+        steps.append((lt_in.at[0, rows], lt_v.at[rows], lt_out.at[0, rows]))
+    steps.append((hvp_in, hvp_v, hvp_out))
+    fetched = [pltpu.make_async_copy(a, b, in_sem.at[i]) for i, (a, b, _) in enumerate(steps)]
+    stored = [pltpu.make_async_copy(b, c, out_sem.at[i]) for i, (_, b, c) in enumerate(steps)]
+    for copy in fetched:
+        copy.start()
+    for first, second in zip(fetched, stored):
+        first.wait()
+        second.start()
+    for copy in stored:
+        copy.wait()
+
+
 def on_device(*args):
     lengths, others = args[6], args[:6] + args[7:]
     dma = pltpu.SemaphoreType.DMA
     vmem = pltpu.VMEM
-    return pl.pallas_call(
+    shapes = (
+        jax.ShapeDtypeStruct((1, TOK, 2048), BF16),
+        jax.ShapeDtypeStruct((32, 1024), F32),
+    )
+    results = pl.pallas_call(
         kernel,
         name="tangent",
-        out_shape=(
-            jax.ShapeDtypeStruct((1, TOK, 2048), BF16),
-            jax.ShapeDtypeStruct((32, 1024), F32),
-        ),
+        out_shape=shapes,
         in_specs=[pl.BlockSpec(memory_space=pltpu.SMEM)] + [pl.BlockSpec(memory_space=pl.ANY)] * 8,
         out_specs=(pl.BlockSpec(memory_space=vmem), pl.BlockSpec(memory_space=vmem)),
         scratch_shapes=[
@@ -385,6 +403,15 @@
             collective_id=0, has_side_effects=True, vmem_limit_bytes=60 * 1024 * 1024
         ),
     )(lengths, *others)
+    anywhere = pl.BlockSpec(memory_space=pl.ANY)
+    return pl.pallas_call(
+        hand_over,
+        name="hand_over",
+        out_shape=shapes,
+        in_specs=[anywhere] * 2,
+        out_specs=(anywhere, anywhere),
+        scratch_shapes=[vmem((TOK, 2048), BF16), vmem((32, 1024), F32), dma((5,)), dma((5,))],
+    )(*results)
 
 
 def solution(mesh):

time: 59.6 us -> 58 us (0.973)
  local copies, waits for them, and re-layouts: 3.45 us -> 0 us
  Pallas kernels: 55.3 us -> 57.2 us
    unnamed x2 -> x0, local copies, waits for them, and re-layouts: 3.45 us -> none
    pallas_call x1 -> x2, Pallas kernels: 55.3 us -> 57.2 us  [the longest x1 55.3 us: on_device(): pl.pallas_call(kernel, name='tangent', out_shape=shapes, in_specs=[pl.Blo...]
where the time goes in v3:
time: 58 us; the launch traced here: 57.8 us
  Pallas kernels  57.2 us (99%)
  between operations  0.64 us (1%)
    pallas_call x1, Pallas kernels, on_device(): pl.pallas_call(kernel, name='tangent', out_shape=shapes, in_specs=[pl.Blo...  55.3 us
    pallas_call x1, Pallas kernels, on_device(): pl.pallas_call(hand_over, name='hand_over', out_shape=shapes, in_specs=[a...  1.91 us

profile of v3, /device:TPU:1, one launch (start us, length us, event | category | flops | bytes accessed | tf_op | source)
XLA Modules:
  0.0 57.8 jit_solution(7153945701784551798)
XLA Ops:
  0.6 55.3 %tangent.1 = (bf16[1,128,2048]{2,1,0:T(8,128)(2,1)}, f32[32,1024]{1,0:T(8,128)}) custom-call(s32[1,17]{1,0:T(1,128)} %len_ref.1, bf16[1,128,1024]{2,1,0:T(8,128)(2,1)} %q_hbm.1, bf16[1,128,256]{2,1,0:T(8,128)(2,1)} %k_hbm.1, bf16[1,128,256]{2,1,0:T(8,128)(2,1)} %v_hbm.1, bf16[1,128,1024]{2,1,0:T(8,128)(2,1)} %dq_hbm.1, bf16[1,128,256]{2,1,0:T(8,128)(2,1)} %dk_hbm.1, ...), custom_call_target="tpu_custom_call" | custom-call | tf_op jit(solution)/shard_map/tangent/pallas_call | solution.py:367
  55.9 1.9 %hand_over.1 = (bf16[1,128,2048]{2,1,0:T(8,128)(2,1)}, f32[32,1024]{1,0:T(8,128)}) custom-call(bf16[1,128,2048]{2,1,0:T(8,128)(2,1)} %get-tuple-element.4.lt_in, f32[32,1024]{1,0:T(8,128)} %get-tuple-element.5.hvp_in), custom_call_target="tpu_custom_call" | custom-call | tf_op jit(solution)/shard_map/hand_over/pallas_call | solution.py:407
